TPU v7x, 1024 devices: a whole 8x8x8 slice. The times are simulated.
1024 devices in a mesh: ctx: 64 (over y, x), head: 16 (over z, core).
Axes of the slice: x: 8, y: 8, z: 8, core: 2. Of those that a mesh axis runs over, the one named last changes fastest.
Arguments:
- queries: bfloat16 [4096, 128, 192], P('ctx', 'head'), may hold values from -84 to 84
- latent_keys: bfloat16 [4096, 576], P('ctx'), may hold values from -12 to 12
- out_grad: bfloat16 [4096, 128, 128], P('ctx', 'head'), may hold values from -6 to 6
- up_weight: bfloat16 [512, 128, 256], P(None, 'head'), may hold values from -0.25 to 0.25
- segment_ids: int32 [4096], replicated, may hold values from 0 to 127, never falling along the last dimension, each value on 1 to 64 neighbouring positions
Outputs:
- query_grad: float32 [4096, 128, 192], P('ctx', 'head')
- key_grad: float32 [4096, 576], P('ctx', 'head')
- weight_grad: float32 [512, 128, 256], P('ctx', 'head')
Inputs may be any that keep to these rules, and one draw needn't show every extreme that they name: `segment_ids`: segment numbers never fall along the slab; each trace has 1 to 64 tokens and one has exactly 64.
All inputs are finite; a program needn't handle non-finite values.
Results may differ from a plain program's by a relative error of at most 0.0053.
Values may be sent and summed in bfloat16 or wider, within the bound.
A program may use at most 32 MiB of HBM per device.

v0:
```python
import math

import jax
import jax.numpy as jnp
from jax import lax
from jax.sharding import PartitionSpec as P

LAT = 512
ROPE = 64
PLAIN_WIDTH = 128
VDIM = 128
REACH = 1


def from_behind(value, axis, steps):
    count = lax.axis_size(axis)
    initial, last = (max(0, -steps), min(count, count - steps))
    return lax.ppermute(value, axis, [(source, source + steps) for source in range(initial, last)])


def shards(queries, latent_keys, out_grad, up_weight, segment_ids):
    tok = latent_keys.shape[0]
    heads = queries.shape[1]
    width = (REACH + 1) * tok
    here = lax.axis_index("ctx")
    scale = 1.0 / math.sqrt(PLAIN_WIDTH + ROPE)
    flat_weight = up_weight.reshape(LAT, heads * (PLAIN_WIDTH + VDIM))
    earlier = [from_behind(latent_keys, "ctx", REACH - 0)]
    window = jnp.concatenate(earlier + [latent_keys], 0)
    kv_win = jnp.dot(window[:, :LAT], flat_weight, preferred_element_type=jnp.float32).astype(
        jnp.bfloat16
    )
    pad_seg = jnp.concatenate([jnp.full((REACH * tok,), -1, jnp.int32), segment_ids], 0)
    seg_keys = lax.dynamic_slice_in_dim(pad_seg, here * tok, width, 0)
    seg_query = lax.dynamic_slice_in_dim(segment_ids, here * tok, tok, 0)
    pos_key = jnp.arange(width)[None, :]
    pos_query = (jnp.arange(tok) + REACH * tok)[:, None]
    visible = (seg_query[:, None] == seg_keys[None, :]) & (pos_key <= pos_query)
    kv_heads = kv_win.reshape(width, heads, PLAIN_WIDTH + VDIM)
    plain_key_part = kv_heads[..., :PLAIN_WIDTH]
    values = kv_heads[..., PLAIN_WIDTH:]
    k_rope = window[:, LAT:]
    q_nope = queries[..., :PLAIN_WIDTH]
    q_rope = queries[..., PLAIN_WIDTH:]
    attention_logits = jnp.einsum(
        "qhd,khd->hqk", q_nope, plain_key_part, preferred_element_type=jnp.float32
    )
    attention_logits = attention_logits + jnp.einsum(
        "qhd,kd->hqk", q_rope, k_rope, preferred_element_type=jnp.float32
    )
    attention_logits = jnp.where(visible[None], attention_logits * scale, -1e30)
    top = jnp.max(attention_logits, -1, keepdims=True)
    expo = jnp.where(visible[None], jnp.exp(attention_logits - top), 0.0)
    probs = expo / jnp.sum(expo, -1, keepdims=True)
    dprobs = jnp.einsum("qhd,khd->hqk", out_grad, values, preferred_element_type=jnp.float32)
    delta = jnp.sum(probs * dprobs, -1, keepdims=True)
    logit_gradient = (probs * (dprobs - delta) * scale).astype(jnp.bfloat16)
    probs16 = probs.astype(jnp.bfloat16)
    grad_nope = jnp.einsum(
        "hqk,khd->qhd", logit_gradient, plain_key_part, preferred_element_type=jnp.float32
    )
    grad_rope = jnp.einsum(
        "hqk,kd->qhd", logit_gradient, k_rope, preferred_element_type=jnp.float32
    )
    query_grad = jnp.concatenate([grad_nope, grad_rope], -1)
    dk_nope = jnp.einsum("hqk,qhd->khd", logit_gradient, q_nope, preferred_element_type=jnp.float32)
    dvalues = jnp.einsum("hqk,qhd->khd", probs16, out_grad, preferred_element_type=jnp.float32)
    dkey_rope = jnp.einsum(
        "hqk,qhd->kd", logit_gradient, q_rope, preferred_element_type=jnp.float32
    )
    dkv = (
        jnp.concatenate([dk_nope, dvalues], -1)
        .astype(jnp.bfloat16)
        .reshape(width, heads * (PLAIN_WIDTH + VDIM))
    )
    dlatent = jnp.einsum("ke,ie->ki", dkv, flat_weight, preferred_element_type=jnp.float32)
    key_terms = jnp.concatenate([dlatent, dkey_rope], -1)
    columns = lax.slice_in_dim(
        window, 0, LAT // lax.axis_size("ctx") * lax.axis_size("ctx"), axis=1
    )
    term = jnp.einsum("ki,ke->ie", columns, dkv, preferred_element_type=jnp.float32)
    weight_rows = lax.psum_scatter(
        lax.optimization_barrier(term.astype(jnp.bfloat16)).astype(jnp.float32),
        "ctx",
        scatter_dimension=0,
        tiled=True,
    )
    weight_grad = weight_rows.reshape(weight_rows.shape[0], heads, PLAIN_WIDTH + VDIM)
    pieces = key_terms.reshape(REACH + 1, tok, LAT + ROPE)
    total = pieces[REACH]
    total = total + from_behind(pieces[0], "ctx", 0 - REACH)
    key_grad = lax.psum_scatter(total, "head", scatter_dimension=1, tiled=True)
    return (query_grad, key_grad, weight_grad)


def solution(mesh):
    return jax.shard_map(
        shards,
        mesh=mesh,
        in_specs=(
            P("ctx", "head", None),
            P("ctx", None),
            P("ctx", "head", None),
            P(None, "head", None),
            P(),
        ),
        out_specs=(P("ctx", "head", None), P("ctx", "head"), P("ctx", "head", None)),
        check_vma=False,
    )
```

profile of v0, /device:TPU:1, one launch (start us, length us, event | category | flops | bytes accessed | tf_op | source)
XLA Modules:
  0.0 508.8 jit_solution(1541810206639285361)
XLA Ops:
  7.2 1.1 copy.23
  8.3 3.9 collective-permute-start
  12.2 0.8 pad_dynamic-slice_fusion
  13.0 0.8 dynamic_slice.6
  13.9 0.9 slice.29
  14.8 0.9 slice.31
  15.7 1.3 dynamic-slice.2
  17.0 1.3 dynamic-slice
  18.3 2.3 copy.48
  23.6 1.8 convolution_bitcast_fusion
  25.5 2.6 convolution_bitcast_fusion.7
  28.1 4.4 convolution_bitcast_fusion.2
  32.4 4.6 convolution_bitcast_fusion.1
  37.1 4.2 convolution_bitcast_fusion.5
  41.3 1.9 fusion.5
  43.3 0.7 pad_maximum_fusion.1
  43.9 1.3 collective-permute-start.1
  45.2 0.8 convolution_convert_fusion
  46.0 278.5 %all-reduce.7 = f32[512,2048]{1,0:T(8,128)} all-reduce(bf16[512,2048]{1,0:T(8,128)(2,1)S(1)} %convolution_convert_fusion), channel_id=3, replica_groups=mesh['ctx'=64,'head'=16] {'ctx'}, use_global_device_ids=true, to_apply=%region_4.5.clone | all-reduce | flops 1048576 | bytes 6291456
  324.5 0.8 constant_dynamic-slice_fusion
  326.1 1.1 copy.35
  327.9 172.4 %all-reduce.6.cloned.1.call-done = f32[64,576]{1,0:T(8,128)} async-done(((f32[64,576]{1,0:T(8,128)}), f32[64,576]{1,0:T(8,128)}) %all-reduce.6.cloned.1.call-update) | async-done | bytes 147472
  500.3 0.9 constant_dynamic-slice_fusion.1
  501.2 0.7 copy.36
  (32 shorter events, 3.3 us)
Async XLA Ops:
  7.2 16.2 %copy-start = (bf16[64,8,128]{2,1,0:T(8,128)(2,1)S(1)}, bf16[64,8,128]{2,1,0:T(8,128)(2,1)}, u32[]{:S(2)}) copy-start(bf16[64,8,128]{2,1,0:T(8,128)(2,1)} %param.7) | copy-start | bytes 393220
  7.2 493.1 %all-reduce.6.cloned.1.call-start = ((), (), s32[]{:S(2)}) async-start(), calls=%async_computation | async-start | bytes 327680
  8.3 13.6 %collective-permute-start = (bf16[64,576]{0,1:T(8,128)(2,1)S(1)}, bf16[64,576]{0,1:T(8,128)(2,1)S(1)}, u32[]{:S(2)}, u32[]{:S(2)}) collective-permute-start(bf16[64,576]{0,1:T(8,128)(2,1)S(1)} %copy.23), channel_id=1, source_target_pairs={{0,16},{16,32},{32,48},{48,64},{64,80},{80,96},{96,112},{112,128},... | collective-permute-start | bytes 221192 | tf_op jit(solution)/shard_map/ppermute | solution.py:18
  23.6 1.8 copy-start.2
  28.1 13.3 %copy-start.1 = (bf16[512,8,256]{2,1,0:T(8,128)(2,1)S(1)}, bf16[512,8,256]{2,1,0:T(8,128)(2,1)}, u32[]{:S(2)}) copy-start(bf16[512,8,256]{2,1,0:T(8,128)(2,1)} %param.8) | copy-start | bytes 6291460
  32.4 8.9 %copy-start.5 = (bf16[128,8,128]{0,2,1:T(8,128)(2,1)S(1)}, bf16[128,8,128]{0,2,1:T(8,128)(2,1)}, u32[]{:S(2)}) copy-start(bf16[128,8,128]{0,2,1:T(8,128)(2,1)} %convolution_bitcast_fusion) | copy-start | bytes 786436
  41.3 1.9 copy-start.6
  43.9 281.4 %collective-permute-start.1 = (f32[64,576]{1,0:T(8,128)}, f32[64,576]{1,0:T(8,128)S(1)}, u32[]{:S(2)}, u32[]{:S(2)}) collective-permute-start(f32[64,576]{1,0:T(8,128)} %pad_maximum_fusion.1), channel_id=1, source_target_pairs={{16,0},{32,16},{48,32},{64,48},{80,64},{96,80},{112,96},{128,112},... | collective-permute-start | bytes 442376 | tf_op jit(solution)/shard_map/ppermute | solution.py:18
  46.0 280.1 %copy-start.3 = (f32[64,8,128]{2,0,1:T(8,128)S(1)}, f32[64,8,128]{2,0,1:T(8,128)}, u32[]{:S(2)}) copy-start(f32[64,8,128]{2,0,1:T(8,128)} %convolution_bitcast_fusion.2) | copy-start | bytes 786436
  46.0 280.1 %copy-start.4 = (f32[64,8,64]{2,0,1:T(8,128)S(1)}, f32[64,8,64]{2,0,1:T(8,128)}, u32[]{:S(2)}) copy-start(f32[64,8,64]{2,0,1:T(8,128)} %convolution_bitcast_fusion.5) | copy-start | bytes 393220
Sparse Core Ops, SparseCore 0:
  326.2 174.0 all-reduce.5
where the time goes:
time: 509 us
  blocking collectives  278 us (55%)
  waiting for transfers between devices  172 us (34%)
  matrix products  21.5 us (4%)
  between operations  15.6 us (3%)
  local copies, waits for them, and re-layouts  13.6 us (3%)
  starting transfers between devices  5.26 us (1%)
    unnamed x1, blocking collectives  278 us
    unnamed x2, waiting for transfers between devices  172 us
    unnamed x24, local copies, waits for them, and re-layouts  10.2 us
  transfers between devices with their start and end apart: 3, of which 1 were waited for; matrix products, arithmetic and copies ran while one was open for 2% of the time, Pallas kernels for 0%

commit v1 on v0

v1 whole, which is shorter than its diff:
```python
import math

import jax
import jax.numpy as jnp
from jax import lax
from jax.experimental import pallas as pl
from jax.experimental.pallas import tpu as pltpu
from jax.sharding import PartitionSpec as P

LAT = 512
ROPE = 64
NOPE = 128
VDIM = 128
KVD = NOPE + VDIM
TOK = 64
WIN = 128
HD = 8
L = 8
NH = 16
KROWS = 48
MESH = pl.DeviceIdType.MESH
F32 = jnp.float32
BF16 = jnp.bfloat16

STEPS = ((4, 0), (3, 1), (3, 0), (2, 1), (2, 0), (1, 1), (1, 0))


def dot(a, b, ca, cb):
    return lax.dot_general(a, b, (((ca,), (cb,)), ((), ())), preferred_element_type=F32)


def kernel(
    q_hbm, lat_hbm, do_hbm, w_hbm, seg_hbm,
    dq_hbm, kg_hbm, wg_hbm,
    q_v, do_v, w_v, seg_v, latwin,
    wf, wflat, qf, dof, dqf, dq_v,
    kv_v, dkv_v, ds_v, qr_v, kt32, kt16,
    term, ring, fin, part, kr, kpart, kprev, kg_v, wgf, wg_v,
    in_sem, halo_sem, ring_send, ring_recv, p2_send, p2_recv, k_send, k_recv, kp_sem, out_sem,
):
    c = lax.axis_index("ctx")
    h = lax.axis_index("head")
    y = lax.div(c, L)
    x = lax.rem(c, L)
    nxt = lax.rem(c + 1, L * L)
    prv = lax.rem(c + L * L - 1, L * L)

    def ctx_of(yy, xx):
        return yy * L + xx

    lat_cp = pltpu.make_async_copy(lat_hbm, latwin.at[pl.ds(TOK, TOK)], in_sem.at[0])
    w_cp = pltpu.make_async_copy(w_hbm, w_v, in_sem.at[1])
    q_cp = pltpu.make_async_copy(q_hbm, q_v, in_sem.at[2])
    do_cp = pltpu.make_async_copy(do_hbm, do_v, in_sem.at[3])
    seg_cp = pltpu.make_async_copy(seg_hbm, seg_v, in_sem.at[4])
    for cp in (lat_cp, w_cp, q_cp, do_cp, seg_cp):
        cp.start()

    barrier = pltpu.get_barrier_semaphore()
    pl.semaphore_signal(barrier, inc=1, device_id=(nxt, h), device_id_type=MESH)
    pl.semaphore_signal(barrier, inc=1, device_id=(prv, h), device_id_type=MESH)
    for d in range(1, L):
        pl.semaphore_signal(
            barrier, inc=1, device_id=(ctx_of(y, lax.rem(x + d, L)), h), device_id_type=MESH
        )
        pl.semaphore_signal(
            barrier, inc=1, device_id=(ctx_of(lax.rem(y + d, L), x), h), device_id_type=MESH
        )
    for d in range(1, NH):
        pl.semaphore_signal(
            barrier, inc=1, device_id=(c, lax.rem(h + d, NH)), device_id_type=MESH
        )

    q_cp.wait()
    do_cp.wait()
    qf[1] = jnp.zeros((TOK * HD, 128), F32)
    qf[0] = q_v[:, :NOPE].astype(F32)
    qf[1, :, :ROPE] = q_v[:, NOPE:].astype(F32)
    dof[...] = do_v[...].astype(F32)
    qn, dob = [], []
    for hd in range(HD):
        qn.append(qf[0, pl.ds(hd, TOK, stride=HD), :].astype(BF16))
        qr_v[pl.ds(hd * TOK, TOK), :] = qf[1, pl.ds(hd, TOK, stride=HD), :].astype(BF16)
        dob.append(dof[pl.ds(hd, TOK, stride=HD), :].astype(BF16))

    lat_cp.wait()
    pl.semaphore_wait(barrier, 2 + 2 * (L - 1) + NH - 1)
    halo = pltpu.make_async_remote_copy(
        src_ref=latwin.at[pl.ds(TOK, TOK)],
        dst_ref=latwin.at[pl.ds(0, TOK)],
        send_sem=halo_sem.at[0],
        recv_sem=halo_sem.at[1],
        device_id=(nxt, h),
        device_id_type=MESH,
    )
    halo.start()

    w_cp.wait()
    rows = LAT * HD // 8

    def relayout(i, carry):
        base = pl.multiple_of(i * rows, rows)
        out = pl.multiple_of(i * (LAT // 8), LAT // 8)
        for half in range(2):
            wf[half] = w_v[pl.ds(base, rows), half * 128 : (half + 1) * 128].astype(F32)
        for hd in range(HD):
            for half in range(2):
                wflat[hd, pl.ds(out, LAT // 8), half * 128 : (half + 1) * 128] = wf[
                    half, pl.ds(hd, LAT // 8, stride=HD), :
                ].astype(BF16)
        return carry

    lax.fori_loop(0, 8, relayout, 0)

    seg_cp.wait()
    row = lax.div(c, 2)
    odd = lax.rem(c, 2)
    lane = lax.broadcasted_iota(jnp.int32, (1, WIN), 1)
    row_a = seg_v[pl.ds(row, 1), :]
    row_b = seg_v[pl.ds(jnp.maximum(row - 1, 0), 1), :]
    mixed = pltpu.roll(jnp.where(lane >= TOK, row_b, row_a), TOK, 1)
    seg_row = jnp.where(odd == 1, row_a, mixed)
    seg_row = jnp.where((lane < TOK) & (c == 0), -1, seg_row).astype(F32)
    seg_all = jnp.broadcast_to(seg_row, (WIN, WIN))
    seg_col = seg_all.T[TOK:, :]
    seg_all = seg_all[:TOK, :]
    pos_key = lax.broadcasted_iota(jnp.int32, (TOK, WIN), 1)
    pos_query = lax.broadcasted_iota(jnp.int32, (TOK, WIN), 0) + TOK
    visible = (seg_col == seg_all) & (pos_key <= pos_query)

    for hd in range(HD):
        kv_v[hd, TOK:, :] = dot(latwin[TOK:, :LAT], wflat[hd], 1, 0).astype(BF16)
    halo.wait_recv()
    for hd in range(HD):
        kv_v[hd, :TOK, :] = dot(latwin[:TOK, :LAT], wflat[hd], 1, 0).astype(BF16)

    k_rope = jnp.concatenate([latwin[:, LAT:], jnp.zeros((WIN, 128 - ROPE), BF16)], 1)
    scale = 1.0 / math.sqrt(NOPE + ROPE)
    scores, dprobs = [], []
    for hd in range(HD):
        key = kv_v[hd, :, :NOPE]
        val = kv_v[hd, :, NOPE:]
        q_rope = qr_v[pl.ds(hd * TOK, TOK), :]
        scores.append(dot(qn[hd], key, 1, 1) + dot(q_rope, k_rope, 1, 1))
        dprobs.append(dot(dob[hd], val, 1, 1))
    for hd in range(HD):
        s = jnp.where(visible, scores[hd] * scale, -1e30)
        top = jnp.max(s, -1, keepdims=True)
        expo = jnp.where(visible, jnp.exp(s - top), 0.0)
        probs = expo / jnp.sum(expo, -1, keepdims=True)
        delta = jnp.sum(probs * dprobs[hd], -1, keepdims=True)
        ds = (probs * (dprobs[hd] - delta) * scale).astype(BF16)
        p16 = probs.astype(BF16)
        ds_v[pl.ds(hd * TOK, TOK), :] = ds
        dkv_v[hd, :, :NOPE] = dot(ds, qn[hd], 0, 0).astype(BF16)
        dkv_v[hd, :, NOPE:] = dot(p16, dob[hd], 0, 0).astype(BF16)

    lat_t = latwin[:, :LAT].T

    def terms(part_id):
        for side in range(2):
            a = 4 * part_id + side
            lo = dot(lat_t, dkv_v[a], 1, 0).reshape(L * L, 8, KVD)
            hi = dot(lat_t, dkv_v[a + 2], 1, 0).reshape(L * L, 8, KVD)
            both = jnp.concatenate([lo, hi], 1).astype(BF16).reshape(L, L, 16, KVD)
            for i in range(L):
                block = both[:, i] if part_id == 0 else both[i]
                term[part_id, i, :, :, side * KVD : (side + 1) * KVD] = block

    def place(part_id, sign, dist):
        pos = x if part_id == 0 else y
        return lax.rem(pos + sign * dist + L, L)

    def neighbour(part_id, sign):
        if part_id == 0:
            return (ctx_of(y, lax.rem(x + sign + L, L)), h)
        return (ctx_of(lax.rem(y + sign + L, L), x), h)

    def message(g, m):
        part_id, back = g // 2, g % 2
        sign = -1 if back else 1
        dist, half = STEPS[m]
        half = half ^ back
        src = term.at[part_id, place(part_id, sign, dist), pl.ds(4 * half, 4)]
        dst = fin.at[g, pl.ds(4 * half, 4)] if dist == 1 else ring.at[g, m]
        return pltpu.make_async_remote_copy(
            src_ref=src,
            dst_ref=dst,
            send_sem=ring_send.at[g, m],
            recv_sem=ring_recv.at[g, m],
            device_id=neighbour(part_id, sign),
            device_id_type=MESH,
        )

    def add(g, m):
        part_id, back = g // 2, g % 2
        sign = -1 if back else 1
        dist, half = STEPS[m]
        half = half ^ back
        at = place(part_id, sign, dist)
        own = term[part_id, at, pl.ds(4 * half, 4)].astype(F32)
        term[part_id, at, pl.ds(4 * half, 4)] = (own + ring[g, m - 2].astype(F32)).astype(BF16)

    for part_id in range(2):
        terms(part_id)
        for g in (2 * part_id, 2 * part_id + 1):
            message(g, 0).start()
            message(g, 1).start()

    acc = dot(wflat[0], dkv_v[0], 1, 1)
    for hd in range(1, HD):
        acc = acc + dot(wflat[hd], dkv_v[hd], 1, 1)
    kt32[pl.ds(0, LAT), :] = acc
    kt32[pl.ds(LAT, ROPE), :] = dot(qr_v[...], ds_v[...], 0, 0)[:ROPE, :]
    kt16[...] = kt32[...].astype(BF16)

    def k_start(to):
        return pl.multiple_of(lax.div(36 * to, 16) * 16, 16)

    k_copies = []
    for d in range(1, NH):
        to = lax.rem(h + d, NH)
        cp = pltpu.make_async_remote_copy(
            src_ref=kt16.at[pl.ds(k_start(to), KROWS)],
            dst_ref=kr.at[d],
            send_sem=k_send.at[d],
            recv_sem=k_recv.at[d],
            device_id=(c, to),
            device_id_type=MESH,
        )
        cp.start()
        k_copies.append(cp)

    for m in range(2, 4):
        for g in range(4):
            message(g, m - 2).wait_recv()
            add(g, m)
            message(g, m).start()

    for hd in range(HD):
        ds = ds_v[pl.ds(hd * TOK, TOK), :]
        dqf[0, pl.ds(hd, TOK, stride=HD), :] = dot(ds, kv_v[hd, :, :NOPE], 1, 0)
        dqf[1, pl.ds(hd, TOK, stride=HD), :] = dot(ds, k_rope, 1, 0)
    dq_v[:, :NOPE] = dqf[0]
    dq_v[:, NOPE:] = dqf[1, :, :ROPE]
    dq_out = pltpu.make_async_copy(dq_v, dq_hbm, out_sem.at[0])
    dq_out.start()

    for m in range(4, 5):
        for g in range(4):
            message(g, m - 2).wait_recv()
            add(g, m)
            message(g, m).start()

    total = kt32[pl.ds(k_start(h), KROWS), :]
    for d in range(1, NH):
        k_copies[d - 1].wait_recv()
        total = total + kr[d].astype(F32)
    kpart[...] = total
    kp = pltpu.make_async_remote_copy(
        src_ref=kpart,
        dst_ref=kprev,
        send_sem=kp_sem.at[0],
        recv_sem=kp_sem.at[1],
        device_id=(prv, h),
        device_id_type=MESH,
    )
    kp.start()

    for m in range(5, 7):
        for g in range(4):
            message(g, m - 2).wait_recv()
            add(g, m)
            message(g, m).start()

    kp.wait_recv()
    both = kpart[...] + pltpu.roll(kprev[...], TOK, 1)
    flip = jnp.concatenate([both, jnp.zeros((128 - KROWS, 128), F32)], 0).T[TOK:, :]
    off = lax.rem(36 * h, 16)
    pick = flip
    for o in (4, 8, 12):
        pick = jnp.where(off == o, pltpu.roll(flip, 128 - o, 1), pick)
    kg_v[...] = pick[:, :36]
    kg_out = pltpu.make_async_copy(kg_v, kg_hbm, out_sem.at[1])
    kg_out.start()

    def p2(part_id, to, frm):
        dev = (ctx_of(to, x), h) if part_id == 0 else (ctx_of(y, to), h)
        return pltpu.make_async_remote_copy(
            src_ref=term.at[part_id, x if part_id == 0 else y, to],
            dst_ref=part.at[part_id, frm],
            send_sem=p2_send.at[part_id, to],
            recv_sem=p2_recv.at[part_id, frm],
            device_id=dev,
            device_id_type=MESH,
        )

    for part_id in range(2):
        mine = x if part_id == 0 else y
        pos = y if part_id == 0 else x
        for back in range(2):
            for m in (5, 6):
                message(2 * part_id + back, m).wait_recv()
        wgf[part_id] = (
            term[part_id, mine, pos].astype(F32)
            + fin[2 * part_id, pos].astype(F32)
            + fin[2 * part_id + 1, pos].astype(F32)
        )
        summed = (
            term[part_id, mine].astype(F32)
            + fin[2 * part_id].astype(F32)
            + fin[2 * part_id + 1].astype(F32)
        )
        term[part_id, mine] = summed.astype(BF16)
        for d in range(1, L):
            p2(part_id, lax.rem(pos + d, L), pos).start()

    for part_id in range(2):
        pos = y if part_id == 0 else x
        total = wgf[part_id]
        for d in range(1, L):
            frm = lax.rem(pos + d, L)
            p2(part_id, frm, frm).wait_recv()
            total = total + part[part_id, frm].astype(F32)
        for a in range(4):
            rows0 = (a // 2) * 8
            for half in range(2):
                cols = (a % 2) * KVD + half * 128
                wg_v[half, pl.ds(4 * part_id + a, 8, stride=HD), :] = total[
                    rows0 : rows0 + 8, cols : cols + 128
                ]
    wg_outs = []
    for half in range(2):
        cp = pltpu.make_async_copy(
            wg_v.at[half], wg_hbm.at[:, pl.ds(half * 128, 128)], out_sem.at[2 + half]
        )
        cp.start()
        wg_outs.append(cp)

    halo.wait_send()
    kp.wait_send()
    for cp in k_copies:
        cp.wait_send()
    for g in range(4):
        for m in range(len(STEPS)):
            message(g, m).wait_send()
    for part_id in range(2):
        pos = y if part_id == 0 else x
        for d in range(1, L):
            p2(part_id, lax.rem(pos + d, L), pos).wait_send()
    for cp in (dq_out, kg_out, *wg_outs):
        cp.wait()


def shards(queries, latent_keys, out_grad, up_weight, segment_ids):
    vm, dma = pltpu.VMEM, pltpu.SemaphoreType.DMA
    dq, kg, wg = pl.pallas_call(
        kernel,
        out_shape=(
            jax.ShapeDtypeStruct((TOK * HD, NOPE + ROPE), F32),
            jax.ShapeDtypeStruct((TOK, 36), F32),
            jax.ShapeDtypeStruct((64, KVD), F32),
        ),
        in_specs=[pl.BlockSpec(memory_space=pl.ANY)] * 5,
        out_specs=[pl.BlockSpec(memory_space=pl.ANY)] * 3,
        scratch_shapes=[
            vm((TOK * HD, NOPE + ROPE), BF16),
            vm((TOK * HD, VDIM), BF16),
            vm((LAT * HD, KVD), BF16),
            vm((32, 128), jnp.int32),
            vm((WIN, LAT + ROPE), BF16),
            vm((2, LAT, 128), F32),
            vm((HD, LAT, KVD), BF16),
            vm((2, TOK * HD, 128), F32),
            vm((TOK * HD, VDIM), F32),
            vm((2, TOK * HD, 128), F32),
            vm((TOK * HD, NOPE + ROPE), F32),
            vm((HD, WIN, KVD), BF16),
            vm((HD, WIN, KVD), BF16),
            vm((HD * TOK, WIN), BF16),
            vm((HD * TOK, 128), BF16),
            vm((LAT + ROPE, WIN), F32),
            vm((LAT + ROPE, WIN), BF16),
            vm((2, L, L, 16, 512), BF16),
            vm((4, 5, 4, 16, 512), BF16),
            vm((4, L, 16, 512), BF16),
            vm((2, L, 16, 512), BF16),
            vm((NH, KROWS, WIN), BF16),
            vm((KROWS, WIN), F32),
            vm((KROWS, WIN), F32),
            vm((TOK, 36), F32),
            vm((2, 16, 512), F32),
            vm((2, 64, 128), F32),
            dma((5,)),
            dma((2,)),
            dma((4, 7)),
            dma((4, 7)),
            dma((2, L)),
            dma((2, L)),
            dma((NH,)),
            dma((NH,)),
            dma((2,)),
            dma((4,)),
        ],
        compiler_params=pltpu.CompilerParams(collective_id=0, has_side_effects=True),
        name="mla_backward",
    )(
        queries.reshape(TOK * HD, NOPE + ROPE),
        latent_keys,
        out_grad.reshape(TOK * HD, VDIM),
        up_weight.reshape(LAT * HD, KVD),
        segment_ids.reshape(32, 128),
    )
    return (
        dq.reshape(TOK, HD, NOPE + ROPE),
        kg,
        wg.reshape(8, HD, KVD),
    )


def solution(mesh):
    return jax.shard_map(
        shards,
        mesh=mesh,
        in_specs=(
            P("ctx", "head", None),
            P("ctx", None),
            P("ctx", "head", None),
            P(None, "head", None),
            P(),
        ),
        out_specs=(P("ctx", "head", None), P("ctx", "head"), P("ctx", "head", None)),
        check_vma=False,
    )
```

time: 509 us -> 56.9 us (0.11)
  the two profiles are of different devices: /device:TPU:1 before, /device:TPU:2 now
where the time goes in v1:
time: 56.9 us; the launch traced here: 56.5 us
  Pallas kernels  51.1 us (90%)
  local copies, waits for them, and re-layouts  4.79 us (8%)
  between operations  0.64 us (1%)
    pallas_call x1, Pallas kernels, shards(): pl.pallas_call(kernel, out_shape=(jax.ShapeDtypeStruct((TOK * HD, NOPE +...  51.1 us
    unnamed x3, local copies, waits for them, and re-layouts  4.79 us

profile of v1, /device:TPU:2, one launch (start us, length us, event | category | flops | bytes accessed | tf_op | source)
XLA Modules:
  0.0 56.5 jit_solution(12469206504733937448)
XLA Ops:
  0.6 51.1 %mla_backward.1 = (f32[512,192]{1,0:T(8,128)}, f32[64,36]{1,0:T(8,128)}, f32[64,256]{1,0:T(8,128)}) custom-call(bf16[512,192]{1,0:T(8,128)(2,1)} %bitcast.8, bf16[64,576]{1,0:T(8,128)(2,1)} %lat_hbm.1, bf16[512,128]{1,0:T(8,128)(2,1)} %bitcast.9, bf16[4096,256]{1,0:T(8,128)(2,1)} %bitcast.6, s32[32,128]{1,0:T(8,128)} %bitcast.11), custom_call_target="tpu_custom_call" | custom-call | tf_op jit(solution)/shard_map/mla_backward/pallas_call | solution.py:357
  51.7 1.4 %copy.8 = f32[64,36]{0,1:T(8,128)} copy(f32[64,36]{1,0:T(8,128)} %get-tuple-element.10) | data formatting | bytes 18432
  53.2 1.9 %copy.11 = f32[64,8,192]{2,1,0:T(8,128)} copy(f32[64,8,192]{2,1,0:T(8,128)} %bitcast.7) | data formatting | bytes 786432
  55.1 1.5 %copy.12 = f32[8,8,256]{2,1,0:T(8,128)} copy(f32[8,8,256]{2,1,0:T(8,128)} %bitcast.10) | data formatting | bytes 131072

commit v2 on v1

--- a/solution.py
+++ b/solution.py
@@ -22,7 +22,11 @@
 F32 = jnp.float32
 BF16 = jnp.bfloat16
 
-STEPS = ((4, 0), (3, 1), (3, 0), (2, 1), (2, 0), (1, 1), (1, 0))
+STEPS = (
+    (4, 0), (4, 1), (3, 2), (3, 3), (3, 0), (3, 1), (2, 2),
+    (2, 3), (2, 0), (2, 1), (1, 2), (1, 3), (1, 0), (1, 1),
+)
+LAG = 4
 
 
 def dot(a, b, ca, cb):
@@ -31,12 +35,12 @@
 
 def kernel(
     q_hbm, lat_hbm, do_hbm, w_hbm, seg_hbm,
-    dq_hbm, kg_hbm, wg_hbm,
+    dq_v, kg_v, wg_v,
     q_v, do_v, w_v, seg_v, latwin,
-    wf, wflat, qf, dof, dqf, dq_v,
+    wf, wflat, qf, dof, dqf,
     kv_v, dkv_v, ds_v, qr_v, kt32, kt16,
-    term, ring, fin, part, kr, kpart, kprev, kg_v, wgf, wg_v,
-    in_sem, halo_sem, ring_send, ring_recv, p2_send, p2_recv, k_send, k_recv, kp_sem, out_sem,
+    term, ring, fin, part, kr, kpart, kprev, wgf, wgs,
+    plane_sem, z_sem, in_sem, halo_sem, ring_send, ring_recv, p2_send, p2_recv, k_send, k_recv, kp_sem,
 ):
     c = lax.axis_index("ctx")
     h = lax.axis_index("head")
@@ -56,19 +60,26 @@
     for cp in (lat_cp, w_cp, q_cp, do_cp, seg_cp):
         cp.start()
 
+    core = lax.rem(h, 2)
+    z = lax.div(h, 2)
+    chip0, chip1 = (c, 2 * z), (c, 2 * z + 1)
     barrier = pltpu.get_barrier_semaphore()
-    pl.semaphore_signal(barrier, inc=1, device_id=(nxt, h), device_id_type=MESH)
-    pl.semaphore_signal(barrier, inc=1, device_id=(prv, h), device_id_type=MESH)
+    for to in (nxt, prv):
+        pl.semaphore_signal(barrier, inc=1, device_id=(to, 2 * z), device_id_type=MESH)
     for d in range(1, L):
+        for to in (ctx_of(y, lax.rem(x + d, L)), ctx_of(lax.rem(y + d, L), x)):
+            pl.semaphore_signal(barrier, inc=1, device_id=(to, 2 * z), device_id_type=MESH)
+
+    @pl.when(core == 1)
+    def _():
+        pl.semaphore_signal(barrier, inc=1, device_id=chip0, device_id_type=MESH)
+
+    for d in range(1, NH // 2):
         pl.semaphore_signal(
-            barrier, inc=1, device_id=(ctx_of(y, lax.rem(x + d, L)), h), device_id_type=MESH
-        )
-        pl.semaphore_signal(
-            barrier, inc=1, device_id=(ctx_of(lax.rem(y + d, L), x), h), device_id_type=MESH
-        )
-    for d in range(1, NH):
-        pl.semaphore_signal(
-            barrier, inc=1, device_id=(c, lax.rem(h + d, NH)), device_id_type=MESH
+            barrier,
+            inc=1,
+            device_id=(c, 2 * lax.rem(z + d, NH // 2) + 1),
+            device_id_type=MESH,
         )
 
     q_cp.wait()
@@ -84,7 +95,16 @@
         dob.append(dof[pl.ds(hd, TOK, stride=HD), :].astype(BF16))
 
     lat_cp.wait()
-    pl.semaphore_wait(barrier, 2 + 2 * (L - 1) + NH - 1)
+
+    @pl.when(core == 0)
+    def _():
+        pl.semaphore_wait(barrier, 2 * (2 + 2 * (L - 1)) + 1)
+        pl.semaphore_signal(plane_sem, inc=1, device_id=chip1, device_id_type=MESH)
+
+    @pl.when(core == 1)
+    def _():
+        pl.semaphore_wait(plane_sem, 1)
+
     halo = pltpu.make_async_remote_copy(
         src_ref=latwin.at[pl.ds(TOK, TOK)],
         dst_ref=latwin.at[pl.ds(0, TOK)],
@@ -179,10 +199,10 @@
     def message(g, m):
         part_id, back = g // 2, g % 2
         sign = -1 if back else 1
-        dist, half = STEPS[m]
-        half = half ^ back
-        src = term.at[part_id, place(part_id, sign, dist), pl.ds(4 * half, 4)]
-        dst = fin.at[g, pl.ds(4 * half, 4)] if dist == 1 else ring.at[g, m]
+        dist, quarter = STEPS[m]
+        quarter = quarter ^ (2 * back)
+        src = term.at[part_id, place(part_id, sign, dist), pl.ds(2 * quarter, 2)]
+        dst = fin.at[g, pl.ds(2 * quarter, 2)] if dist == 1 else ring.at[g, m]
         return pltpu.make_async_remote_copy(
             src_ref=src,
             dst_ref=dst,
@@ -195,17 +215,26 @@
     def add(g, m):
         part_id, back = g // 2, g % 2
         sign = -1 if back else 1
-        dist, half = STEPS[m]
-        half = half ^ back
+        dist, quarter = STEPS[m]
+        quarter = quarter ^ (2 * back)
         at = place(part_id, sign, dist)
-        own = term[part_id, at, pl.ds(4 * half, 4)].astype(F32)
-        term[part_id, at, pl.ds(4 * half, 4)] = (own + ring[g, m - 2].astype(F32)).astype(BF16)
+        own = term[part_id, at, pl.ds(2 * quarter, 2)].astype(F32)
+        term[part_id, at, pl.ds(2 * quarter, 2)] = (own + ring[g, m - LAG].astype(F32)).astype(
+            BF16
+        )
+
+    def advance(lo, hi):
+        for m in range(lo, hi):
+            for g in range(4):
+                message(g, m - LAG).wait_recv()
+                add(g, m)
+                message(g, m).start()
 
     for part_id in range(2):
         terms(part_id)
         for g in (2 * part_id, 2 * part_id + 1):
-            message(g, 0).start()
-            message(g, 1).start()
+            for m in range(LAG):
+                message(g, m).start()
 
     acc = dot(wflat[0], dkv_v[0], 1, 1)
     for hd in range(1, HD):
@@ -217,10 +246,9 @@
     def k_start(to):
         return pl.multiple_of(lax.div(36 * to, 16) * 16, 16)
 
-    k_copies = []
-    for d in range(1, NH):
+    def k_copy(d):
         to = lax.rem(h + d, NH)
-        cp = pltpu.make_async_remote_copy(
+        return pltpu.make_async_remote_copy(
             src_ref=kt16.at[pl.ds(k_start(to), KROWS)],
             dst_ref=kr.at[d],
             send_sem=k_send.at[d],
@@ -228,14 +256,21 @@
             device_id=(c, to),
             device_id_type=MESH,
         )
-        cp.start()
-        k_copies.append(cp)
-
-    for m in range(2, 4):
-        for g in range(4):
-            message(g, m - 2).wait_recv()
-            add(g, m)
-            message(g, m).start()
+
+    def k_exchange():
+        @pl.when(core == 1)
+        def _():
+            pl.semaphore_wait(barrier, NH - 2)
+            pl.semaphore_signal(z_sem, inc=1, device_id=chip0, device_id_type=MESH)
+
+        @pl.when(core == 0)
+        def _():
+            pl.semaphore_wait(z_sem, 1)
+
+        for d in range(1, NH):
+            k_copy(d).start()
+
+    pl.when(z >= 4)(k_exchange)
 
     for hd in range(HD):
         ds = ds_v[pl.ds(hd * TOK, TOK), :]
@@ -243,18 +278,54 @@
         dqf[1, pl.ds(hd, TOK, stride=HD), :] = dot(ds, k_rope, 1, 0)
     dq_v[:, :NOPE] = dqf[0]
     dq_v[:, NOPE:] = dqf[1, :, :ROPE]
-    dq_out = pltpu.make_async_copy(dq_v, dq_hbm, out_sem.at[0])
-    dq_out.start()
-
-    for m in range(4, 5):
+
+    advance(LAG, 10)
+    pl.when(z < 4)(k_exchange)
+    advance(10, len(STEPS))
+
+    def p2(part_id, to, frm):
+        dev = (ctx_of(to, x), h) if part_id == 0 else (ctx_of(y, to), h)
+        return pltpu.make_async_remote_copy(
+            src_ref=term.at[part_id, x if part_id == 0 else y, to],
+            dst_ref=part.at[part_id, frm],
+            send_sem=p2_send.at[part_id, to],
+            recv_sem=p2_recv.at[part_id, frm],
+            device_id=dev,
+            device_id_type=MESH,
+        )
+
+    def finish(part_id, quarter):
+        mine = x if part_id == 0 else y
+        pos = y if part_id == 0 else x
+        at = pl.ds(2 * quarter, 2)
+        summed = (
+            term[part_id, mine, at].astype(F32)
+            + fin[2 * part_id, at].astype(F32)
+            + fin[2 * part_id + 1, at].astype(F32)
+        )
+        term[part_id, mine, at] = summed.astype(BF16)
+        for j in range(2):
+            to = 2 * quarter + j
+
+            @pl.when(pos == to)
+            def _():
+                wgf[part_id] = summed[j]
+
+            @pl.when(pos != to)
+            def _():
+                p2(part_id, to, pos).start()
+
+    for last in range(2):
         for g in range(4):
-            message(g, m - 2).wait_recv()
-            add(g, m)
-            message(g, m).start()
+            message(g, 10 + last).wait_recv()
+            message(g, 12 + last).wait_recv()
+        for part_id in range(2):
+            finish(part_id, last)
+            finish(part_id, 2 + last)
 
     total = kt32[pl.ds(k_start(h), KROWS), :]
     for d in range(1, NH):
-        k_copies[d - 1].wait_recv()
+        k_copy(d).wait_recv()
         total = total + kr[d].astype(F32)
     kpart[...] = total
     kp = pltpu.make_async_remote_copy(
@@ -267,54 +338,6 @@
     )
     kp.start()
 
-    for m in range(5, 7):
-        for g in range(4):
-            message(g, m - 2).wait_recv()
-            add(g, m)
-            message(g, m).start()
-
-    kp.wait_recv()
-    both = kpart[...] + pltpu.roll(kprev[...], TOK, 1)
-    flip = jnp.concatenate([both, jnp.zeros((128 - KROWS, 128), F32)], 0).T[TOK:, :]
-    off = lax.rem(36 * h, 16)
-    pick = flip
-    for o in (4, 8, 12):
-        pick = jnp.where(off == o, pltpu.roll(flip, 128 - o, 1), pick)
-    kg_v[...] = pick[:, :36]
-    kg_out = pltpu.make_async_copy(kg_v, kg_hbm, out_sem.at[1])
-    kg_out.start()
-
-    def p2(part_id, to, frm):
-        dev = (ctx_of(to, x), h) if part_id == 0 else (ctx_of(y, to), h)
-        return pltpu.make_async_remote_copy(
-            src_ref=term.at[part_id, x if part_id == 0 else y, to],
-            dst_ref=part.at[part_id, frm],
-            send_sem=p2_send.at[part_id, to],
-            recv_sem=p2_recv.at[part_id, frm],
-            device_id=dev,
-            device_id_type=MESH,
-        )
-
-    for part_id in range(2):
-        mine = x if part_id == 0 else y
-        pos = y if part_id == 0 else x
-        for back in range(2):
-            for m in (5, 6):
-                message(2 * part_id + back, m).wait_recv()
-        wgf[part_id] = (
-            term[part_id, mine, pos].astype(F32)
-            + fin[2 * part_id, pos].astype(F32)
-            + fin[2 * part_id + 1, pos].astype(F32)
-        )
-        summed = (
-            term[part_id, mine].astype(F32)
-            + fin[2 * part_id].astype(F32)
-            + fin[2 * part_id + 1].astype(F32)
-        )
-        term[part_id, mine] = summed.astype(BF16)
-        for d in range(1, L):
-            p2(part_id, lax.rem(pos + d, L), pos).start()
-
     for part_id in range(2):
         pos = y if part_id == 0 else x
         total = wgf[part_id]
@@ -326,21 +349,24 @@
             rows0 = (a // 2) * 8
             for half in range(2):
                 cols = (a % 2) * KVD + half * 128
-                wg_v[half, pl.ds(4 * part_id + a, 8, stride=HD), :] = total[
+                wgs[half, pl.ds(4 * part_id + a, 8, stride=HD), :] = total[
                     rows0 : rows0 + 8, cols : cols + 128
                 ]
-    wg_outs = []
-    for half in range(2):
-        cp = pltpu.make_async_copy(
-            wg_v.at[half], wg_hbm.at[:, pl.ds(half * 128, 128)], out_sem.at[2 + half]
-        )
-        cp.start()
-        wg_outs.append(cp)
+    wg_v[:, :128] = wgs[0]
+    wg_v[:, 128:] = wgs[1]
+
+    kp.wait_recv()
+    both = pltpu.roll(kpart[...], TOK, 1) + kprev[...]
+    off = lax.rem(36 * h, 16)
+    pick = both
+    for o in (4, 8, 12):
+        pick = jnp.where(off == o, pltpu.roll(both, KROWS - o, 0), pick)
+    kg_v[...] = pick[:36, :TOK]
 
     halo.wait_send()
     kp.wait_send()
-    for cp in k_copies:
-        cp.wait_send()
+    for d in range(1, NH):
+        k_copy(d).wait_send()
     for g in range(4):
         for m in range(len(STEPS)):
             message(g, m).wait_send()
@@ -348,7 +374,16 @@
         pos = y if part_id == 0 else x
         for d in range(1, L):
             p2(part_id, lax.rem(pos + d, L), pos).wait_send()
-    for cp in (dq_out, kg_out, *wg_outs):
+
+
+def hand_out(dq, kg, wg, dq_to, kg_to, wg_to, sem):
+    copies = [
+        pltpu.make_async_copy(src, dst, sem.at[i])
+        for i, (src, dst) in enumerate(((dq, dq_to), (kg, kg_to), (wg, wg_to)))
+    ]
+    for cp in copies:
+        cp.start()
+    for cp in copies:
         cp.wait()
 
 
@@ -358,11 +393,11 @@
         kernel,
         out_shape=(
             jax.ShapeDtypeStruct((TOK * HD, NOPE + ROPE), F32),
-            jax.ShapeDtypeStruct((TOK, 36), F32),
+            jax.ShapeDtypeStruct((36, TOK), F32),
             jax.ShapeDtypeStruct((64, KVD), F32),
         ),
-        in_specs=[pl.BlockSpec(memory_space=pl.ANY)] * 5,
-        out_specs=[pl.BlockSpec(memory_space=pl.ANY)] * 3,
+        in_specs=[pl.BlockSpec(memory_space=pltpu.HBM)] * 5,
+        out_specs=[pl.BlockSpec(memory_space=pltpu.VMEM)] * 3,
         scratch_shapes=[
             vm((TOK * HD, NOPE + ROPE), BF16),
             vm((TOK * HD, VDIM), BF16),
@@ -374,7 +409,6 @@
             vm((2, TOK * HD, 128), F32),
             vm((TOK * HD, VDIM), F32),
             vm((2, TOK * HD, 128), F32),
-            vm((TOK * HD, NOPE + ROPE), F32),
             vm((HD, WIN, KVD), BF16),
             vm((HD, WIN, KVD), BF16),
             vm((HD * TOK, WIN), BF16),
@@ -382,38 +416,54 @@
             vm((LAT + ROPE, WIN), F32),
             vm((LAT + ROPE, WIN), BF16),
             vm((2, L, L, 16, 512), BF16),
-            vm((4, 5, 4, 16, 512), BF16),
+            vm((4, 10, 2, 16, 512), BF16),
             vm((4, L, 16, 512), BF16),
             vm((2, L, 16, 512), BF16),
             vm((NH, KROWS, WIN), BF16),
             vm((KROWS, WIN), F32),
             vm((KROWS, WIN), F32),
-            vm((TOK, 36), F32),
             vm((2, 16, 512), F32),
             vm((2, 64, 128), F32),
+            pltpu.SemaphoreType.REGULAR,
+            pltpu.SemaphoreType.REGULAR,
             dma((5,)),
             dma((2,)),
-            dma((4, 7)),
-            dma((4, 7)),
+            dma((4, len(STEPS))),
+            dma((4, len(STEPS))),
             dma((2, L)),
             dma((2, L)),
             dma((NH,)),
             dma((NH,)),
             dma((2,)),
-            dma((4,)),
         ],
-        compiler_params=pltpu.CompilerParams(collective_id=0, has_side_effects=True),
+        compiler_params=pltpu.CompilerParams(
+            collective_id=0, has_side_effects=True, vmem_limit_bytes=32 * 1024 * 1024
+        ),
         name="mla_backward",
     )(
-        queries.reshape(TOK * HD, NOPE + ROPE),
-        latent_keys,
-        out_grad.reshape(TOK * HD, VDIM),
-        up_weight.reshape(LAT * HD, KVD),
-        segment_ids.reshape(32, 128),
+        *(
+            pltpu.with_memory_space_constraint(a, pltpu.HBM)
+            for a in (
+                queries.reshape(TOK * HD, NOPE + ROPE),
+                latent_keys,
+                out_grad.reshape(TOK * HD, VDIM),
+                up_weight.reshape(LAT * HD, KVD),
+                segment_ids.reshape(32, 128),
+            )
+        )
     )
+    dq, kg, wg = pl.pallas_call(
+        hand_out,
+        out_shape=tuple(jax.ShapeDtypeStruct(a.shape, a.dtype) for a in (dq, kg, wg)),
+        in_specs=[pl.BlockSpec(memory_space=pl.ANY)] * 3,
+        out_specs=[pl.BlockSpec(memory_space=pl.ANY)] * 3,
+        scratch_shapes=[dma((3,))],
+        compiler_params=pltpu.CompilerParams(vmem_limit_bytes=8 * 1024 * 1024),
+        name="hand_out",
+    )(dq, kg, wg)
     return (
         dq.reshape(TOK, HD, NOPE + ROPE),
-        kg,
+        kg.T,
         wg.reshape(8, HD, KVD),
     )
 

time: 56.9 us -> 46.5 us (0.82)
  the two profiles are of different devices: /device:TPU:2 before, /device:TPU:32 now
where the time goes in v2:
time: 46.5 us; the launch traced here: 46.4 us
  Pallas kernels  45.7 us (98%)
  between operations  0.64 us (1%)
    pallas_call x1, Pallas kernels, shards(): pl.pallas_call(kernel, out_shape=(jax.ShapeDtypeStruct((TOK * HD, NOPE +...  44.9 us

profile of v2, /device:TPU:32, one launch (start us, length us, event | category | flops | bytes accessed | tf_op | source)
XLA Modules:
  0.0 46.4 jit_solution(12727684829996863423)
XLA Ops:
  0.6 44.9 %mla_backward.1 = (f32[512,192]{1,0:T(8,128)S(1)}, f32[36,64]{1,0:T(8,128)S(1)}, f32[64,256]{1,0:T(8,128)S(1)}) custom-call(bf16[512,192]{1,0:T(8,128)(2,1)} %bitcast.8, bf16[64,576]{1,0:T(8,128)(2,1)} %lat_hbm.1, bf16[512,128]{1,0:T(8,128)(2,1)} %bitcast.9, bf16[4096,256]{1,0:T(8,128)(2,1)} %bitcast.7, s32[32,128]{1,0:T(8,128)} %bitcast.10), custom_call_target="tpu_custom_call" | custom-call | tf_op jit(solution)/shard_map/mla_backward/pallas_call | solution.py:392
  45.5 0.8 %hand_out.1 = (f32[512,192]{1,0:T(8,128)}, f32[36,64]{1,0:T(8,128)}, f32[64,256]{1,0:T(8,128)}) custom-call(f32[512,192]{1,0:T(8,128)S(1)} %get-tuple-element.9.dq, f32[36,64]{1,0:T(8,128)S(1)} %get-tuple-element.10.kg, f32[64,256]{1,0:T(8,128)S(1)} %get-tuple-element.11.wg), custom_call_target="tpu_custom_call" | custom-call | tf_op jit(solution)/shard_map/hand_out/pallas_call | solution.py:455

commit v3 on v2

--- a/solution.py
+++ b/solution.py
@@ -57,18 +57,18 @@
     q_cp = pltpu.make_async_copy(q_hbm, q_v, in_sem.at[2])
     do_cp = pltpu.make_async_copy(do_hbm, do_v, in_sem.at[3])
     seg_cp = pltpu.make_async_copy(seg_hbm, seg_v, in_sem.at[4])
-    for cp in (lat_cp, w_cp, q_cp, do_cp, seg_cp):
+    for cp in (lat_cp, q_cp, do_cp, seg_cp, w_cp):
         cp.start()
 
     core = lax.rem(h, 2)
     z = lax.div(h, 2)
     chip0, chip1 = (c, 2 * z), (c, 2 * z + 1)
     barrier = pltpu.get_barrier_semaphore()
-    for to in (nxt, prv):
+    near = [nxt, prv]
+    for d in (1, L - 1):
+        near += [ctx_of(y, lax.rem(x + d, L)), ctx_of(lax.rem(y + d, L), x)]
+    for to in near:
         pl.semaphore_signal(barrier, inc=1, device_id=(to, 2 * z), device_id_type=MESH)
-    for d in range(1, L):
-        for to in (ctx_of(y, lax.rem(x + d, L)), ctx_of(lax.rem(y + d, L), x)):
-            pl.semaphore_signal(barrier, inc=1, device_id=(to, 2 * z), device_id_type=MESH)
 
     @pl.when(core == 1)
     def _():
@@ -81,6 +81,35 @@
             device_id=(c, 2 * lax.rem(z + d, NH // 2) + 1),
             device_id_type=MESH,
         )
+
+    lat_cp.wait()
+
+    @pl.when(core == 0)
+    def _():
+        pl.semaphore_wait(barrier, 2 * len(near) + 1)
+        pl.semaphore_signal(plane_sem, inc=1, device_id=chip1, device_id_type=MESH)
+
+    @pl.when(core == 1)
+    def _():
+        pl.semaphore_wait(plane_sem, 1)
+
+    halo = pltpu.make_async_remote_copy(
+        src_ref=latwin.at[pl.ds(TOK, TOK)],
+        dst_ref=latwin.at[pl.ds(0, TOK)],
+        send_sem=halo_sem.at[0],
+        recv_sem=halo_sem.at[1],
+        device_id=(nxt, h),
+        device_id_type=MESH,
+    )
+    first, final = c == 0, c == L * L - 1
+
+    @pl.when(jnp.logical_not(final))
+    def _():
+        halo.start()
+
+    @pl.when(first)
+    def _():
+        latwin[:TOK, :] = jnp.zeros((TOK, LAT + ROPE), BF16)
 
     q_cp.wait()
     do_cp.wait()
@@ -93,27 +122,6 @@
         qn.append(qf[0, pl.ds(hd, TOK, stride=HD), :].astype(BF16))
         qr_v[pl.ds(hd * TOK, TOK), :] = qf[1, pl.ds(hd, TOK, stride=HD), :].astype(BF16)
         dob.append(dof[pl.ds(hd, TOK, stride=HD), :].astype(BF16))
-
-    lat_cp.wait()
-
-    @pl.when(core == 0)
-    def _():
-        pl.semaphore_wait(barrier, 2 * (2 + 2 * (L - 1)) + 1)
-        pl.semaphore_signal(plane_sem, inc=1, device_id=chip1, device_id_type=MESH)
-
-    @pl.when(core == 1)
-    def _():
-        pl.semaphore_wait(plane_sem, 1)
-
-    halo = pltpu.make_async_remote_copy(
-        src_ref=latwin.at[pl.ds(TOK, TOK)],
-        dst_ref=latwin.at[pl.ds(0, TOK)],
-        send_sem=halo_sem.at[0],
-        recv_sem=halo_sem.at[1],
-        device_id=(nxt, h),
-        device_id_type=MESH,
-    )
-    halo.start()
 
     w_cp.wait()
     rows = LAT * HD // 8
@@ -150,7 +158,11 @@
 
     for hd in range(HD):
         kv_v[hd, TOK:, :] = dot(latwin[TOK:, :LAT], wflat[hd], 1, 0).astype(BF16)
-    halo.wait_recv()
+
+    @pl.when(jnp.logical_not(first))
+    def _():
+        halo.wait_recv()
+
     for hd in range(HD):
         kv_v[hd, :TOK, :] = dot(latwin[:TOK, :LAT], wflat[hd], 1, 0).astype(BF16)
 
@@ -336,7 +348,10 @@
         device_id=(prv, h),
         device_id_type=MESH,
     )
-    kp.start()
+
+    @pl.when(jnp.logical_not(first))
+    def _():
+        kp.start()
 
     for part_id in range(2):
         pos = y if part_id == 0 else x
@@ -355,7 +370,14 @@
     wg_v[:, :128] = wgs[0]
     wg_v[:, 128:] = wgs[1]
 
-    kp.wait_recv()
+    @pl.when(jnp.logical_not(final))
+    def _():
+        kp.wait_recv()
+
+    @pl.when(final)
+    def _():
+        kprev[...] = jnp.zeros((KROWS, WIN), F32)
+
     both = pltpu.roll(kpart[...], TOK, 1) + kprev[...]
     off = lax.rem(36 * h, 16)
     pick = both
@@ -363,8 +385,14 @@
         pick = jnp.where(off == o, pltpu.roll(both, KROWS - o, 0), pick)
     kg_v[...] = pick[:36, :TOK]
 
-    halo.wait_send()
-    kp.wait_send()
+    @pl.when(jnp.logical_not(final))
+    def _():
+        halo.wait_send()
+
+    @pl.when(jnp.logical_not(first))
+    def _():
+        kp.wait_send()
+
     for d in range(1, NH):
         k_copy(d).wait_send()
     for g in range(4):

time: 46.5 us -> 44.4 us (0.955)
  the two profiles are of different devices: /device:TPU:32 before, /device:TPU:4 now
where the time goes in v3:
time: 44.4 us; the launch traced here: 44.2 us
  Pallas kernels  43.6 us (98%)
  between operations  0.64 us (1%)
    pallas_call x1, Pallas kernels, shards(): pl.pallas_call(kernel, out_shape=(jax.ShapeDtypeStruct((TOK * HD, NOPE +...  42.7 us

profile of v3, /device:TPU:4, one launch (start us, length us, event | category | flops | bytes accessed | tf_op | source)
XLA Modules:
  0.0 44.2 jit_solution(12010326505543149184)
XLA Ops:
  0.6 42.7 %mla_backward.1 = (f32[512,192]{1,0:T(8,128)S(1)}, f32[36,64]{1,0:T(8,128)S(1)}, f32[64,256]{1,0:T(8,128)S(1)}) custom-call(bf16[512,192]{1,0:T(8,128)(2,1)} %bitcast.8, bf16[64,576]{1,0:T(8,128)(2,1)} %lat_hbm.1, bf16[512,128]{1,0:T(8,128)(2,1)} %bitcast.9, bf16[4096,256]{1,0:T(8,128)(2,1)} %bitcast.7, s32[32,128]{1,0:T(8,128)} %bitcast.10), custom_call_target="tpu_custom_call" | custom-call | tf_op jit(solution)/shard_map/mla_backward/pallas_call | solution.py:420
  43.4 0.8 %hand_out.1 = (f32[512,192]{1,0:T(8,128)}, f32[36,64]{1,0:T(8,128)}, f32[64,256]{1,0:T(8,128)}) custom-call(f32[512,192]{1,0:T(8,128)S(1)} %get-tuple-element.9.dq, f32[36,64]{1,0:T(8,128)S(1)} %get-tuple-element.10.kg, f32[64,256]{1,0:T(8,128)S(1)} %get-tuple-element.11.wg), custom_call_target="tpu_custom_call" | custom-call | tf_op jit(solution)/shard_map/hand_out/pallas_call | solution.py:483

commit v4 on v3

--- a/solution.py
+++ b/solution.py
@@ -235,9 +235,9 @@
             BF16
         )
 
-    def advance(lo, hi):
+    def advance(lo, hi, directions=range(4)):
         for m in range(lo, hi):
-            for g in range(4):
+            for g in directions:
                 message(g, m - LAG).wait_recv()
                 add(g, m)
                 message(g, m).start()
@@ -291,9 +291,30 @@
     dq_v[:, :NOPE] = dqf[0]
     dq_v[:, NOPE:] = dqf[1, :, :ROPE]
 
-    advance(LAG, 10)
-    pl.when(z < 4)(k_exchange)
-    advance(10, len(STEPS))
+    row0 = (h == 0) & (y == 0) & (x > 0)
+    col0 = (h == 0) & (x == 0) & (y > 0)
+
+    def in_turn(first_part):
+        own = (2 * first_part, 2 * first_part + 1)
+        rest = (2 - 2 * first_part, 3 - 2 * first_part)
+        advance(LAG, len(STEPS), own)
+        advance(LAG, 10, rest)
+        k_exchange()
+        advance(10, len(STEPS), rest)
+
+    @pl.when(row0)
+    def _():
+        in_turn(1)
+
+    @pl.when(col0)
+    def _():
+        in_turn(0)
+
+    @pl.when(jnp.logical_not(row0 | col0))
+    def _():
+        advance(LAG, 10)
+        pl.when(z < 4)(k_exchange)
+        advance(10, len(STEPS))
 
     def p2(part_id, to, frm):
         dev = (ctx_of(to, x), h) if part_id == 0 else (ctx_of(y, to), h)

time: 44.4 us -> 51.6 us (1.16)
  Pallas kernels: 43.6 us -> 50.7 us
    pallas_call x1, Pallas kernels: 42.7 us -> 49.9 us  [shards(): pl.pallas_call(kernel, out_shape=(jax.ShapeDtypeStruct((TOK * HD, NOPE +...]
where the time goes in v4:
time: 51.6 us; the launch traced here: 51.4 us
  Pallas kernels  50.7 us (98%)
  between operations  0.64 us (1%)
    pallas_call x1, Pallas kernels, shards(): pl.pallas_call(kernel, out_shape=(jax.ShapeDtypeStruct((TOK * HD, NOPE +...  49.9 us

profile of v4, /device:TPU:4, one launch (start us, length us, event | category | flops | bytes accessed | tf_op | source)
XLA Modules:
  0.0 51.4 jit_solution(5942155468417462366)
XLA Ops:
  0.6 49.9 %mla_backward.1 = (f32[512,192]{1,0:T(8,128)S(1)}, f32[36,64]{1,0:T(8,128)S(1)}, f32[64,256]{1,0:T(8,128)S(1)}) custom-call(bf16[512,192]{1,0:T(8,128)(2,1)} %bitcast.8, bf16[64,576]{1,0:T(8,128)(2,1)} %lat_hbm.1, bf16[512,128]{1,0:T(8,128)(2,1)} %bitcast.9, bf16[4096,256]{1,0:T(8,128)(2,1)} %bitcast.7, s32[32,128]{1,0:T(8,128)} %bitcast.10), custom_call_target="tpu_custom_call" | custom-call | tf_op jit(solution)/shard_map/mla_backward/pallas_call | solution.py:441
  50.6 0.8 %hand_out.1 = (f32[512,192]{1,0:T(8,128)}, f32[36,64]{1,0:T(8,128)}, f32[64,256]{1,0:T(8,128)}) custom-call(f32[512,192]{1,0:T(8,128)S(1)} %get-tuple-element.9.dq, f32[36,64]{1,0:T(8,128)S(1)} %get-tuple-element.10.kg, f32[64,256]{1,0:T(8,128)S(1)} %get-tuple-element.11.wg), custom_call_target="tpu_custom_call" | custom-call | tf_op jit(solution)/shard_map/hand_out/pallas_call | solution.py:504

commit v5 on v3

--- a/solution.py
+++ b/solution.py
@@ -60,36 +60,37 @@
     for cp in (lat_cp, q_cp, do_cp, seg_cp, w_cp):
         cp.start()
 
-    core = lax.rem(h, 2)
+    odd_x = lax.rem(c, 2)
+    even_ctx = c - odd_x
+    odd_ctx = even_ctx + 1
     z = lax.div(h, 2)
-    chip0, chip1 = (c, 2 * z), (c, 2 * z + 1)
     barrier = pltpu.get_barrier_semaphore()
-    near = [nxt, prv]
+
+    def greet(to):
+        gate = to - lax.rem(to, 2)
+
+        @pl.when(gate != c)
+        def _():
+            pl.semaphore_signal(barrier, inc=1, device_id=(gate, h), device_id_type=MESH)
+
+    greet(nxt)
+    greet(prv)
     for d in (1, L - 1):
-        near += [ctx_of(y, lax.rem(x + d, L)), ctx_of(lax.rem(y + d, L), x)]
-    for to in near:
-        pl.semaphore_signal(barrier, inc=1, device_id=(to, 2 * z), device_id_type=MESH)
-
-    @pl.when(core == 1)
-    def _():
-        pl.semaphore_signal(barrier, inc=1, device_id=chip0, device_id_type=MESH)
-
-    for d in range(1, NH // 2):
+        greet(ctx_of(y, lax.rem(x + d, L)))
+        greet(ctx_of(lax.rem(y + d, L), x))
+    for d in range(1, NH):
         pl.semaphore_signal(
-            barrier,
-            inc=1,
-            device_id=(c, 2 * lax.rem(z + d, NH // 2) + 1),
-            device_id_type=MESH,
+            barrier, inc=1, device_id=(odd_ctx, lax.rem(h + d, NH)), device_id_type=MESH
         )
 
     lat_cp.wait()
 
-    @pl.when(core == 0)
-    def _():
-        pl.semaphore_wait(barrier, 2 * len(near) + 1)
-        pl.semaphore_signal(plane_sem, inc=1, device_id=chip1, device_id_type=MESH)
-
-    @pl.when(core == 1)
+    @pl.when(odd_x == 0)
+    def _():
+        pl.semaphore_wait(barrier, 10)
+        pl.semaphore_signal(plane_sem, inc=1, device_id=(odd_ctx, h), device_id_type=MESH)
+
+    @pl.when(odd_x == 1)
     def _():
         pl.semaphore_wait(plane_sem, 1)
 
@@ -169,11 +170,11 @@
     k_rope = jnp.concatenate([latwin[:, LAT:], jnp.zeros((WIN, 128 - ROPE), BF16)], 1)
     scale = 1.0 / math.sqrt(NOPE + ROPE)
     scores, dprobs = [], []
+    s_rope = dot(qr_v[...], k_rope, 1, 1)
     for hd in range(HD):
         key = kv_v[hd, :, :NOPE]
         val = kv_v[hd, :, NOPE:]
-        q_rope = qr_v[pl.ds(hd * TOK, TOK), :]
-        scores.append(dot(qn[hd], key, 1, 1) + dot(q_rope, k_rope, 1, 1))
+        scores.append(dot(qn[hd], key, 1, 1) + s_rope[hd * TOK : (hd + 1) * TOK])
         dprobs.append(dot(dob[hd], val, 1, 1))
     for hd in range(HD):
         s = jnp.where(visible, scores[hd] * scale, -1e30)
@@ -270,12 +271,12 @@
         )
 
     def k_exchange():
-        @pl.when(core == 1)
+        @pl.when(odd_x == 1)
         def _():
-            pl.semaphore_wait(barrier, NH - 2)
-            pl.semaphore_signal(z_sem, inc=1, device_id=chip0, device_id_type=MESH)
-
-        @pl.when(core == 0)
+            pl.semaphore_wait(barrier, 2 * (NH - 1))
+            pl.semaphore_signal(z_sem, inc=1, device_id=(even_ctx, h), device_id_type=MESH)
+
+        @pl.when(odd_x == 0)
         def _():
             pl.semaphore_wait(z_sem, 1)
 

time: 44.4 us -> 44.3 us (level)
  no operation moved by 1% of the time
where the time goes in v5:
time: 44.3 us; the launch traced here: 44.1 us
  Pallas kernels  43.5 us (98%)
  between operations  0.64 us (1%)
    pallas_call x1, Pallas kernels, shards(): pl.pallas_call(kernel, out_shape=(jax.ShapeDtypeStruct((TOK * HD, NOPE +...  42.6 us

profile of v5, /device:TPU:4, one launch (start us, length us, event | category | flops | bytes accessed | tf_op | source)
XLA Modules:
  0.0 44.1 jit_solution(8442761350012098952)
XLA Ops:
  0.6 42.6 %mla_backward.1 = (f32[512,192]{1,0:T(8,128)S(1)}, f32[36,64]{1,0:T(8,128)S(1)}, f32[64,256]{1,0:T(8,128)S(1)}) custom-call(bf16[512,192]{1,0:T(8,128)(2,1)} %bitcast.8, bf16[64,576]{1,0:T(8,128)(2,1)} %lat_hbm.1, bf16[512,128]{1,0:T(8,128)(2,1)} %bitcast.9, bf16[4096,256]{1,0:T(8,128)(2,1)} %bitcast.7, s32[32,128]{1,0:T(8,128)} %bitcast.10), custom_call_target="tpu_custom_call" | custom-call | tf_op jit(solution)/shard_map/mla_backward/pallas_call | solution.py:421
  43.3 0.8 %hand_out.1 = (f32[512,192]{1,0:T(8,128)}, f32[36,64]{1,0:T(8,128)}, f32[64,256]{1,0:T(8,128)}) custom-call(f32[512,192]{1,0:T(8,128)S(1)} %get-tuple-element.9.dq, f32[36,64]{1,0:T(8,128)S(1)} %get-tuple-element.10.kg, f32[64,256]{1,0:T(8,128)S(1)} %get-tuple-element.11.wg), custom_call_target="tpu_custom_call" | custom-call | tf_op jit(solution)/shard_map/hand_out/pallas_call | solution.py:484

commit v6 on v5

--- a/solution.py
+++ b/solution.py
@@ -296,46 +296,6 @@
     pl.when(z < 4)(k_exchange)
     advance(10, len(STEPS))
 
-    def p2(part_id, to, frm):
-        dev = (ctx_of(to, x), h) if part_id == 0 else (ctx_of(y, to), h)
-        return pltpu.make_async_remote_copy(
-            src_ref=term.at[part_id, x if part_id == 0 else y, to],
-            dst_ref=part.at[part_id, frm],
-            send_sem=p2_send.at[part_id, to],
-            recv_sem=p2_recv.at[part_id, frm],
-            device_id=dev,
-            device_id_type=MESH,
-        )
-
-    def finish(part_id, quarter):
-        mine = x if part_id == 0 else y
-        pos = y if part_id == 0 else x
-        at = pl.ds(2 * quarter, 2)
-        summed = (
-            term[part_id, mine, at].astype(F32)
-            + fin[2 * part_id, at].astype(F32)
-            + fin[2 * part_id + 1, at].astype(F32)
-        )
-        term[part_id, mine, at] = summed.astype(BF16)
-        for j in range(2):
-            to = 2 * quarter + j
-
-            @pl.when(pos == to)
-            def _():
-                wgf[part_id] = summed[j]
-
-            @pl.when(pos != to)
-            def _():
-                p2(part_id, to, pos).start()
-
-    for last in range(2):
-        for g in range(4):
-            message(g, 10 + last).wait_recv()
-            message(g, 12 + last).wait_recv()
-        for part_id in range(2):
-            finish(part_id, last)
-            finish(part_id, 2 + last)
-
     total = kt32[pl.ds(k_start(h), KROWS), :]
     for d in range(1, NH):
         k_copy(d).wait_recv()
@@ -353,6 +313,46 @@
     @pl.when(jnp.logical_not(first))
     def _():
         kp.start()
+
+    def p2(part_id, to, frm):
+        dev = (ctx_of(to, x), h) if part_id == 0 else (ctx_of(y, to), h)
+        return pltpu.make_async_remote_copy(
+            src_ref=term.at[part_id, x if part_id == 0 else y, to],
+            dst_ref=part.at[part_id, frm],
+            send_sem=p2_send.at[part_id, to],
+            recv_sem=p2_recv.at[part_id, frm],
+            device_id=dev,
+            device_id_type=MESH,
+        )
+
+    def finish(part_id, quarter):
+        mine = x if part_id == 0 else y
+        pos = y if part_id == 0 else x
+        at = pl.ds(2 * quarter, 2)
+        summed = (
+            term[part_id, mine, at].astype(F32)
+            + fin[2 * part_id, at].astype(F32)
+            + fin[2 * part_id + 1, at].astype(F32)
+        )
+        term[part_id, mine, at] = summed.astype(BF16)
+        for j in range(2):
+            to = 2 * quarter + j
+
+            @pl.when(pos == to)
+            def _():
+                wgf[part_id] = summed[j]
+
+            @pl.when(pos != to)
+            def _():
+                p2(part_id, to, pos).start()
+
+    for last in range(2):
+        for g in range(4):
+            message(g, 10 + last).wait_recv()
+            message(g, 12 + last).wait_recv()
+        for part_id in range(2):
+            finish(part_id, last)
+            finish(part_id, 2 + last)
 
     for part_id in range(2):
         pos = y if part_id == 0 else x

time: 44.3 us -> 44.3 us (level)
  no operation moved by 1% of the time
where the time goes in v6:
time: 44.3 us; the launch traced here: 44.1 us
  Pallas kernels  43.5 us (98%)
  between operations  0.64 us (1%)
    pallas_call x1, Pallas kernels, shards(): pl.pallas_call(kernel, out_shape=(jax.ShapeDtypeStruct((TOK * HD, NOPE +...  42.7 us

profile of v6, /device:TPU:4, one launch (start us, length us, event | category | flops | bytes accessed | tf_op | source)
XLA Modules:
  0.0 44.1 jit_solution(8006085694209268778)
XLA Ops:
  0.6 42.7 %mla_backward.1 = (f32[512,192]{1,0:T(8,128)S(1)}, f32[36,64]{1,0:T(8,128)S(1)}, f32[64,256]{1,0:T(8,128)S(1)}) custom-call(bf16[512,192]{1,0:T(8,128)(2,1)} %bitcast.8, bf16[64,576]{1,0:T(8,128)(2,1)} %lat_hbm.1, bf16[512,128]{1,0:T(8,128)(2,1)} %bitcast.9, bf16[4096,256]{1,0:T(8,128)(2,1)} %bitcast.7, s32[32,128]{1,0:T(8,128)} %bitcast.10), custom_call_target="tpu_custom_call" | custom-call | tf_op jit(solution)/shard_map/mla_backward/pallas_call | solution.py:421
  43.3 0.8 %hand_out.1 = (f32[512,192]{1,0:T(8,128)}, f32[36,64]{1,0:T(8,128)}, f32[64,256]{1,0:T(8,128)}) custom-call(f32[512,192]{1,0:T(8,128)S(1)} %get-tuple-element.9.dq, f32[36,64]{1,0:T(8,128)S(1)} %get-tuple-element.10.kg, f32[64,256]{1,0:T(8,128)S(1)} %get-tuple-element.11.wg), custom_call_target="tpu_custom_call" | custom-call | tf_op jit(solution)/shard_map/hand_out/pallas_call | solution.py:484
